TPU v7x, 32 devices: a whole 2x2x4 slice. The times are simulated.
32 devices in a mesh: groups: 2 (over x), blk: 16 (over z, y, core).
Axes of the slice: x: 2, y: 2, z: 4, core: 2. Of those that a mesh axis runs over, the one named last changes fastest.
Arguments:
- text_queries: bfloat16 [4096, 4096], P(('groups', 'blk')), parts along dimension 0, may hold values from -170 to 170
- image_states: bfloat16 [1536, 8192], P(('groups', 'blk')), parts along dimension 0, may hold values from -6 to 6
- kv_weight: bfloat16 [8192, 1024], P('blk'), may hold values from -0.1875 to 0.1875
- q_gain: float32 [128], replicated, may hold values from 0.25 to 1.75
- k_gain: float32 [128], replicated, may hold values from 0.25 to 1.75
- text_counts: int32 [6], P('groups'), parts along dimension 0, may hold values from 1 to 1024, 2048 in all
- image_counts: int32 [6], P('groups'), parts along dimension 0, may hold values from 96 to 384, as said below
Outputs:
- attended: bfloat16 [4096, 4096], P(('groups', 'blk')), parts along dimension 0
There are 2 independent parts, one for each index of `groups`. A program takes and returns all parts, laid end to end along the dimension named above; an argument that names none is the same for every part. Nothing has to cross between parts.
Inputs may be any that keep to these rules, and one draw needn't show every extreme that they name: `text_counts`: they sum to 2048. `image_counts`: they sum to 768; the second image has exactly 384 tokens, the first and last are cut by the window.
All inputs are finite; a program needn't handle non-finite values.
Results may differ from a plain program's by a relative error of at most 0.0071.
Values may be sent and summed in bfloat16 or wider, within the bound.
No kernel may reach another device: no remote copies, remote signals or barrier semaphores. Data moves between devices by JAX's collectives and lax.ppermute only.
A program may use at most 128 MiB of HBM per device.

v0:
```python
import math
import jax
import jax.numpy as jnp
from jax import lax
from jax.sharding import PartitionSpec as P

epsilon = 1e-05


def rms_norm(inputs, norm_gain):
    return (
        inputs * lax.rsqrt(jnp.mean(inputs * inputs, axis=-1, keepdims=True) + epsilon) * norm_gain
    )


def body(text_queries, image_states, kv_weight, q_gain, k_gain, text_counts, image_counts):
    head_dim = q_gain.shape[0]
    text_rows = text_queries.shape[0]
    image_rows = image_states.shape[0]
    kv_width = kv_weight.shape[1] // 2
    kv_heads = kv_width // head_dim
    query_heads = text_queries.shape[1] // head_dim
    group_size = query_heads // kv_heads
    columns = lax.all_to_all(image_states, "blk", split_axis=1, concat_axis=0, tiled=True)
    projected = lax.psum_scatter(
        jnp.dot(columns, kv_weight, preferred_element_type=jnp.float32),
        "blk",
        scatter_dimension=0,
        tiled=True,
    )
    image_keys = rms_norm(projected[:, :kv_width].reshape(image_rows, kv_heads, head_dim), k_gain)
    image_keys = image_keys.astype(jnp.bfloat16).reshape(image_rows, kv_width)
    image_values = projected[:, kv_width:].astype(jnp.bfloat16)
    kv_rows_local = jnp.concatenate([image_keys, image_values], axis=1)
    normed_queries = rms_norm(
        text_queries.astype(jnp.float32).reshape(text_rows, query_heads, head_dim), q_gain
    )
    normed_queries = normed_queries.astype(jnp.bfloat16).reshape(
        text_rows, kv_heads, group_size, head_dim
    )
    text_positions = lax.axis_index("blk") * text_rows + jnp.arange(text_rows, dtype=jnp.int32)
    text_ends = jnp.cumsum(text_counts)
    image_ends = jnp.cumsum(image_counts)
    text_segment = jnp.sum(
        (text_ends[None, :] <= text_positions[:, None]).astype(jnp.int32), axis=1
    )
    score_scale = 1.0 / math.sqrt(head_dim)
    arrived = lax.all_gather(kv_rows_local, "blk", axis=0, tiled=True)
    first_row = jnp.int32(0)
    numerator = jnp.zeros((kv_heads, group_size, text_rows, head_dim), jnp.float32)
    denominator = jnp.zeros((kv_heads, group_size, text_rows), jnp.float32)
    key_span = arrived.shape[0]
    for offset in range(0, key_span, 512):
        block_size = min(512, key_span - offset)
        key_block = arrived[offset : offset + block_size]
        key_heads = key_block[:, :kv_width].reshape(block_size, kv_heads, head_dim)
        value_heads = key_block[:, kv_width:].reshape(block_size, kv_heads, head_dim)
        key_positions = first_row + offset + jnp.arange(block_size, dtype=jnp.int32)
        key_owner = jnp.sum(
            (image_ends[None, :] <= key_positions[:, None]).astype(jnp.int32), axis=1
        )
        allowed = key_owner[None, :] <= text_segment[:, None]
        scores = (
            jnp.einsum(
                "tgrd,pgd->grtp", normed_queries, key_heads, preferred_element_type=jnp.float32
            )
            * score_scale
        )
        weights = jnp.where(allowed, jnp.exp(scores), 0.0)
        denominator = denominator + jnp.sum(weights, axis=-1)
        numerator = numerator + jnp.einsum(
            "grtp,pgd->grtd",
            weights.astype(jnp.bfloat16),
            value_heads,
            preferred_element_type=jnp.float32,
        )
    numerator, denominator = (numerator, denominator)
    attended = (numerator / denominator[..., None]).astype(jnp.bfloat16)
    return jnp.transpose(attended, (2, 0, 1, 3)).reshape(text_rows, query_heads * head_dim)


def solution(mesh):
    placed = (
        P(("groups", "blk"), None),
        P(("groups", "blk"), None),
        P("blk", None),
        P(),
        P(),
        P("groups"),
        P("groups"),
    )
    return jax.shard_map(
        body, mesh=mesh, in_specs=placed, out_specs=P(("groups", "blk"), None), check_vma=False
    )
```

profile of v0, /device:TPU:0, one launch (start us, length us, event | category | flops | bytes accessed | tf_op | source)
XLA Modules:
  0.0 173.4 jit_solution(13814516155407754564)
XLA Ops:
  6.5 1.3 copy.124
  7.8 27.3 %all_to_all.19 = bf16[48,16,512]{2,0,1:T(8,128)(2,1)S(1)} all-to-all(bf16[48,16,512]{2,0,1:T(8,128)(2,1)S(1)} %bitcast.70), channel_id=1, replica_groups=mesh['groups'=2,'blk'=16] {'blk'}, dimensions={1} | all-to-all | bytes 1572864 | tf_op jit(solution)/shard_map/all_to_all | solution.py:24
  35.2 2.6 %fusion.34 = f32[768,1024]{1,0:T(8,128)} fusion(bf16[768,512]{1,0:T(8,128)(2,1)S(1)} %bitcast.69, bf16[512,1024]{1,0:T(8,128)(2,1)S(1)} %copy-done), kind=kOutput, calls=%fused_computation.51 | convolution fusion | flops 805306368 | bytes 4980736 | tf_op jit(solution)/shard_map/dot_general | solution.py:26
  37.9 0.6 copy-done.4
  38.5 65.1 %reduce-scatter.2.cloned.1.call-done = f32[48,1024]{1,0:T(8,128)} async-done(((f32[768,1024]{1,0:T(8,128)}), f32[48,1024]{1,0:T(8,128)}) %reduce-scatter.2.cloned.1.call-update) | async-done | bytes 196624 | tf_op jit(solution)/shard_map/reduce_scatter | solution.py:25
  103.6 0.9 slice_multiply_fusion
  104.5 0.1 reduce_sum.65
  104.7 0.9 slice.40
  105.7 0.9 fusion.27
  106.6 0.6 pad_maximum_fusion
  107.3 0.2 reduce-window.17
  107.5 0.2 reduce-window.16
  107.7 0.2 fusion.9
  107.9 0.4 copy.101
  108.3 0.6 reduce_sum.66
  108.9 1.4 convert_bitcast_fusion
  110.4 0.4 copy.100
  111.0 0.1 broadcast_compare_fusion.1
  111.2 0.1 broadcast_compare_fusion
  111.3 34.7 %all-gather.2.cloned.1.call-done = bf16[768,1024]{1,0:T(8,128)(2,1)} async-done(((bf16[48,1024]{1,0:T(8,128)(2,1)}), bf16[768,1024]{1,0:T(8,128)(2,1)}) %all-gather.2.cloned.1.call-update) | async-done | bytes 1572880 | tf_op jit(solution)/shard_map/all_gather | solution.py:48
  146.0 2.2 %fusion.32 = (bf16[512,512]{1,0:T(8,128)(2,1)}, bf16[512,512]{1,0:T(8,128)(2,1)}) fusion(bf16[768,1024]{1,0:T(8,128)(2,1)} %all-gather.2.cloned.1.call-done), kind=kLoop, calls=%fused_computation.49 | loop fusion | bytes 2097152 | tf_op jit(solution)/shard_map/slice | solution.py:56
  148.3 2.0 %reshape.123 = bf16[512,4,128]{2,1,0:T(4,128)(2,1)} reshape(bf16[512,512]{1,0:T(8,128)(2,1)} %get-tuple-element.5) | data formatting | bytes 1048576 | tf_op jit(solution)/shard_map/reshape | solution.py:56
  150.2 1.8 %fusion.33 = (bf16[256,512]{1,0:T(8,128)(2,1)S(1)}, bf16[256,512]{1,0:T(8,128)(2,1)}) fusion(bf16[768,1024]{1,0:T(8,128)(2,1)} %all-gather.2.cloned.1.call-done), kind=kLoop, calls=%fused_computation.50 | loop fusion | bytes 1048576 | tf_op jit(solution)/shard_map/slice | solution.py:56
  152.0 0.8 reshape.126
  152.8 1.1 copy.97
  153.9 2.0 %copy.94 = bf16[512,512]{0,1:T(8,128)(2,1)} copy(bf16[512,512]{1,0:T(8,128)(2,1)} %get-tuple-element.6) | data formatting | bytes 1048576 | tf_op jit(solution)/shard_map/reshape | solution.py:57
  155.9 3.2 %fusion.7 = (f32[4,8,128]{2,1,0:T(8,128)S(1)}, f32[4,256,128,8]{2,1,3,0:T(8,128)S(1)}) fusion(pred[128,256]{0,1:T(8,128)(4,1)S(1)} %broadcast_compare_fusion.1, f32[128,4,8,128]{3,2,1,0:T(8,128)S(1)} %bitcast.71, f32[128]{0:T(128)S(1)} %copy-done.7, f32[128,4,8]{0,2,1:T(8,128)S(1)} %rsqrt_bitcast_fusion, bf16[256,4,128,1]{2,1,0,3:T(4,128)(2,1)} %bitcast.79), kind=kOutput, calls=%fused_computation.8 | convolution fusion | flops 273149952 | bytes 6619648 | tf_op jit(solution)/shard_map/tgrd,pgd->grtp/dot_general | solution.py:64
  159.1 0.9 fusion.10
  160.0 0.2 copy-done.2
  160.2 3.3 %fusion = (f32[4,8,128]{2,1,0:T(8,128)S(1)}, f32[4,512,128,8]{2,1,3,0:T(8,128)S(1)}) fusion(pred[128,512]{0,1:T(8,128)(4,1)S(1)} %broadcast_compare_fusion, f32[128,4,8,128]{3,2,1,0:T(8,128)S(1)} %bitcast.72, f32[128]{0:T(128)S(1)} %copy-done.7, f32[128,4,8]{0,2,1:T(8,128)S(1)} %rsqrt_bitcast_fusion, bf16[512,4,128,1]{2,1,0,3:T(4,128)(2,1)S(1)} %bitcast.76), kind=kOutput, calls=%fused_computation.1 | convolution fusion | flops 544731136 | bytes 11108864 | tf_op jit(solution)/shard_map/tgrd,pgd->grtp/dot_general | solution.py:64
  163.5 1.8 %fusion.12 = bf16[128,4,8,128]{0,3,2,1:T(8,128)(2,1)S(1)} fusion(f32[4,8,128,128]{2,3,1,0:T(8,128)S(1)} %fusion.10, bf16[512,4,128,1]{0,2,3,1:T(8,128)(2,1)S(1)} %bitcast.77, f32[4,512,128,8]{2,1,3,0:T(8,128)S(1)} %get-tuple-element.10, pred[128,512]{0,1:T(8,128)(4,1)S(1)} %broadcast_compare_fusion, f32[128,4,8]{0,2,1:T(8,128)S(1)} %add_bitcast_fusion), kind=kOutput, calls=%fused_computation.15 | convolution fusion | flops 544735232 | bytes 12140544 | tf_op jit(solution)/shard_map/grtp,pgd->grtd/dot_general | solution.py:71
  165.3 1.3 copy.85
  (30 shorter events, 0.6 us)
Async XLA Ops:
  6.5 28.6 %copy-start = (bf16[512,1024]{1,0:T(8,128)(2,1)S(1)}, bf16[512,1024]{1,0:T(8,128)(2,1)}, u32[]{:S(2)}) copy-start(bf16[512,1024]{1,0:T(8,128)(2,1)} %param.9) | copy-start | bytes 3145732
  6.5 97.0 %reduce-scatter.2.cloned.1.call-start = ((), (), s32[]{:S(2)}) async-start(), calls=%async_computation.2 | async-start | bytes 3342336 | tf_op jit(solution)/shard_map/reduce_scatter | solution.py:25
  37.8 0.7 copy-start.4
  37.8 69.5 %copy-start.5 = (s32[3]{0:T(128)S(1)}, s32[3]{0:T(128)}, u32[]{:S(2)}) copy-start(s32[3]{0:T(128)} %param.12) | copy-start | bytes 40
  37.8 69.6 %copy-start.6 = (s32[3]{0:T(128)S(1)}, s32[3]{0:T(128)}, u32[]{:S(2)}) copy-start(s32[3]{0:T(128)} %param.13) | copy-start | bytes 40
  37.8 69.8 %copy-start.1 = (bf16[128,4096]{1,0:T(8,128)(2,1)S(1)}, bf16[128,4096]{1,0:T(8,128)(2,1)}, u32[]{:S(2)}) copy-start(bf16[128,4096]{1,0:T(8,128)(2,1)} %param.7) | copy-start | bytes 3145732
  37.9 108.2 %all-gather.2.cloned.1.call-start = ((), (), s32[]{:S(2)}) async-start(), calls=%async_computation.3 | async-start | bytes 1671168 | tf_op jit(solution)/shard_map/all_gather | solution.py:48
  148.3 7.7 %copy-start.7 = (f32[128]{0:T(128)S(1)}, f32[128]{0:T(128)}, u32[]{:S(2)}) copy-start(f32[128]{0:T(128)} %param.10) | copy-start | bytes 1540
  159.1 1.0 copy-start.2
  160.2 3.3 %copy-start.3 = (bf16[512,512]{0,1:T(8,128)(2,1)S(1)}, bf16[512,512]{0,1:T(8,128)(2,1)}, u32[]{:S(2)}) copy-start(bf16[512,512]{0,1:T(8,128)(2,1)} %copy.94) | copy-start | bytes 1572868
Sparse Core Ops, SparseCore 0:
  38.0 65.5 reduce-scatter.1
  107.4 38.5 all-gather.1
where the time goes:
time: 174 us; the launch traced here: 173 us
  waiting for transfers between devices  99.9 us (57%)
  blocking collectives  27.3 us (16%)
  local copies, waits for them, and re-layouts  15.1 us (9%)
  between operations  13.6 us (8%)
  matrix products  11.8 us (7%)
  other arithmetic  5.74 us (3%)
    reduce_scatter x1, waiting for transfers between devices, body(): lax.psum_scatter(jnp.dot(columns, kv_weight, preferred_element_type=jnp.f...  65.1 us
    all_gather x1, waiting for transfers between devices, body(): arrived = lax.all_gather(kv_rows_local, 'blk', axis=0, tiled=True)  34.7 us
    all_to_all x1, blocking collectives, body(): lax.all_to_all(image_states, 'blk', split_axis=1, concat_axis=0, tiled=True)  27.3 us
    dot_general x2, matrix products, body(): jnp.einsum('tgrd,pgd->grtp', normed_queries, key_heads, preferred_element...  6.52 us
    slice x2, local copies, waits for them, and re-layouts, body(): key_heads = key_block[:, :kv_width].reshape(block_size, kv_heads, head_dim)  4 us
  transfers between devices with their start and end apart: 2, of which 2 were waited for; matrix products, arithmetic and copies ran while one was open for 2% of the time, Pallas kernels for 0%

commit v1 on v0

--- a/solution.py
+++ b/solution.py
@@ -45,7 +45,17 @@
         (text_ends[None, :] <= text_positions[:, None]).astype(jnp.int32), axis=1
     )
     score_scale = 1.0 / math.sqrt(head_dim)
-    arrived = lax.all_gather(kv_rows_local, "blk", axis=0, tiled=True)
+    mixed_arr = lax.psum(1, "blk")
+    kept_arr = lax.axis_index("blk")
+    block_now, tmp = (mixed_arr, kept_arr)
+    arrived, v1 = (kv_rows_local, 1)
+    while v1 < block_now:
+        near = tuple(((pp, pp ^ v1) for pp in range(block_now)))
+        all_rows = lax.ppermute(arrived, axis_name="blk", perm=near)
+        raw_out = jnp.concatenate([arrived, all_rows], axis=0)
+        a_now = jnp.concatenate([all_rows, arrived], axis=0)
+        arrived = jnp.where(tmp & v1 == 0, raw_out, a_now)
+        v1 = 2 * v1
     first_row = jnp.int32(0)
     numerator = jnp.zeros((kv_heads, group_size, text_rows, head_dim), jnp.float32)
     denominator = jnp.zeros((kv_heads, group_size, text_rows), jnp.float32)

time: 174 us -> 191 us (1.098)
  other arithmetic: 5.74 us -> 13.9 us
  starting transfers between devices: 0.04 us -> 3.92 us
  waiting for transfers between devices: 99.9 us -> 103 us
    ppermute x0 -> x4, waiting for transfers between devices: none -> 38.3 us  [body(): all_rows = lax.ppermute(arrived, axis_name='blk', perm=near)]
    all_gather x1 -> x0, waiting for transfers between devices: 34.7 us -> none  [body(): arrived = lax.all_gather(kv_rows_local, 'blk', axis=0, tiled=True)]
    ppermute x0 -> x4, starting transfers between devices: none -> 3.92 us  [body(): all_rows = lax.ppermute(arrived, axis_name='blk', perm=near)]
    unnamed x18 -> x26, local copies, waits for them, and re-layouts: 1.5 us -> 4.22 us
    unnamed x2, other arithmetic: 1.66 us -> 4.23 us
    reduce_sum x2, other arithmetic: 0.73 us -> 3.11 us  [rms_norm(): jnp.mean(inputs * inputs, axis=-1, keepdims=True) + epsilon]
    select_n x0 -> x4, other arithmetic: none -> 2.24 us  [body(): arrived = jnp.where(tmp & v1 == 0, raw_out, a_now)]
    slice x2, local copies, waits for them, and re-layouts: 4 us -> 1.81 us  [body(): key_heads = key_block[:, :kv_width].reshape(block_size, kv_heads, head_dim)]
  transfers between devices with their start and end apart: 2 -> 5, of which waited for: 2 -> 4; matrix products, arithmetic and copies ran while one was open for 2% -> 7% of each run, Pallas kernels for 0% -> 0%
where the time goes in v1:
time: 191 us
  waiting for transfers between devices  103 us (54%)
  blocking collectives  27.3 us (14%)
  local copies, waits for them, and re-layouts  16.6 us (9%)
  other arithmetic  13.9 us (7%)
  between operations  13.6 us (7%)
  matrix products  11.8 us (6%)
  starting transfers between devices  3.92 us (2%)
    reduce_scatter x1, waiting for transfers between devices, body(): lax.psum_scatter(jnp.dot(columns, kv_weight, preferred_element_type=jnp.f...  65.1 us
    ppermute x4, waiting for transfers between devices, body(): all_rows = lax.ppermute(arrived, axis_name='blk', perm=near)  38.3 us
    all_to_all x1, blocking collectives, body(): lax.all_to_all(image_states, 'blk', split_axis=1, concat_axis=0, tiled=True)  27.3 us
    dot_general x2, matrix products, body(): jnp.einsum('tgrd,pgd->grtp', normed_queries, key_heads, preferred_element...  6.52 us
    unnamed x2, other arithmetic  4.23 us
    unnamed x26, local copies, waits for them, and re-layouts  4.22 us
    ppermute x4, starting transfers between devices, body(): all_rows = lax.ppermute(arrived, axis_name='blk', perm=near)  3.92 us
  transfers between devices with their start and end apart: 5, of which 4 were waited for; matrix products, arithmetic and copies ran while one was open for 7% of the time, Pallas kernels for 0%

profile of v1, /device:TPU:0, one launch (start us, length us, event | category | flops | bytes accessed | tf_op | source)
XLA Modules:
  0.0 190.5 jit_solution(7807019636808100631)
XLA Ops:
  6.5 1.3 copy.124
  7.8 27.3 %all_to_all.19 = bf16[48,16,512]{2,0,1:T(8,128)(2,1)S(1)} all-to-all(bf16[48,16,512]{2,0,1:T(8,128)(2,1)S(1)} %bitcast.70), channel_id=1, replica_groups=mesh['groups'=2,'blk'=16] {'blk'}, dimensions={1} | all-to-all | bytes 1572864 | tf_op jit(solution)/shard_map/all_to_all | solution.py:24
  35.2 2.6 %fusion.34 = f32[768,1024]{1,0:T(8,128)} fusion(bf16[768,512]{1,0:T(8,128)(2,1)S(1)} %bitcast.69, bf16[512,1024]{1,0:T(8,128)(2,1)S(1)} %copy-done), kind=kOutput, calls=%fused_computation.55 | convolution fusion | flops 805306368 | bytes 4980736 | tf_op jit(solution)/shard_map/dot_general | solution.py:26
  38.5 65.1 %reduce-scatter.2.cloned.1.call-done = f32[48,1024]{1,0:T(8,128)} async-done(((f32[768,1024]{1,0:T(8,128)}), f32[48,1024]{1,0:T(8,128)}) %reduce-scatter.2.cloned.1.call-update) | async-done | bytes 196624 | tf_op jit(solution)/shard_map/reduce_scatter | solution.py:25
  103.6 0.9 slice_multiply_fusion
  104.7 0.9 slice.40
  105.7 0.9 fusion.27
  106.7 1.4 fusion.9
  108.2 1.0 collective-permute-start.1
  109.3 2.8 %convert_bitcast_fusion = f32[16,8,32,128]{3,1,2,0:T(8,128)} fusion(bf16[128,4096]{1,0:T(8,128)(2,1)} %param.7), kind=kLoop, calls=%fused_computation.11 | loop fusion | flops 524288 | bytes 3145728
  112.1 3.5 %collective-permute-done.1 = bf16[96,1024]{1,0:T(8,128)(2,1)S(1)} collective-permute-done((bf16[96,1024]{1,0:T(8,128)(2,1)S(1)}, bf16[96,1024]{1,0:T(8,128)(2,1)S(1)}, u32[]{:S(2)}, u32[]{:S(2)}) %collective-permute-start.1) | collective-permute-done | bytes 196640 | tf_op jit(solution)/shard_map/ppermute | solution.py:54
  115.7 1.3 collective-permute-start.2
  117.5 0.7 reduce-window.17
  118.2 0.7 reduce-window.16
  118.9 1.7 copy.101
  120.6 3.0 %reduce_sum.66 = f32[128,32]{1,0:T(8,128)} reduce(f32[128,32,128]{2,1,0:T(8,128)} %bitcast.68, f32[]{:T(128)} %constant.8.clone.1), dimensions={2}, to_apply=%region_6.7 | reduce | flops 520192 | bytes 2113540 | tf_op jit(solution)/shard_map/reduce_sum | solution.py:12
  123.6 0.9 copy.77
  124.5 1.7 copy.100
  126.5 1.4 maximum_select_fusion.1
  128.0 1.5 collective-permute-start.3
  129.8 34.6 %collective-permute-done.3 = bf16[384,1024]{1,0:T(8,128)(2,1)S(1)} collective-permute-done((bf16[384,1024]{1,0:T(8,128)(2,1)S(1)}, bf16[384,1024]{1,0:T(8,128)(2,1)S(1)}, u32[]{:S(2)}, u32[]{:S(2)}) %collective-permute-start.3) | collective-permute-done | bytes 786464 | tf_op jit(solution)/shard_map/ppermute | solution.py:54
  165.2 0.8 fusion.33
  165.9 1.1 fusion.32
  167.0 2.1 %reshape.123 = bf16[512,4,128]{2,1,0:T(4,128)(2,1)} reshape(bf16[512,512]{1,0:T(8,128)(2,1)} %get-tuple-element.5) | data formatting | bytes 1048576 | tf_op jit(solution)/shard_map/reshape | solution.py:66
  169.1 0.8 reshape.126
  169.9 1.1 copy.97
  170.9 2.0 %copy.94 = bf16[512,512]{0,1:T(8,128)(2,1)} copy(bf16[512,512]{1,0:T(8,128)(2,1)} %get-tuple-element.6) | data formatting | bytes 1048576 | tf_op jit(solution)/shard_map/reshape | solution.py:67
  173.0 3.2 %fusion.7 = (f32[4,8,128]{2,1,0:T(8,128)S(1)}, f32[4,256,128,8]{2,1,3,0:T(8,128)S(1)}) fusion(pred[128,256]{0,1:T(8,128)(4,1)S(1)} %broadcast_compare_fusion.1, f32[128,4,8,128]{3,2,1,0:T(8,128)S(1)} %bitcast.71, f32[128]{0:T(128)S(1)} %copy-done.9, f32[128,4,8]{0,2,1:T(8,128)S(1)} %rsqrt_bitcast_fusion, bf16[256,4,128,1]{2,1,0,3:T(4,128)(2,1)} %bitcast.79), kind=kOutput, calls=%fused_computation.8 | convolution fusion | flops 273149952 | bytes 6619648 | tf_op jit(solution)/shard_map/tgrd,pgd->grtp/dot_general | solution.py:74
  176.2 0.9 fusion.10
  177.3 3.3 %fusion = (f32[4,8,128]{2,1,0:T(8,128)S(1)}, f32[4,512,128,8]{2,1,3,0:T(8,128)S(1)}) fusion(pred[128,512]{0,1:T(8,128)(4,1)S(1)} %broadcast_compare_fusion, f32[128,4,8,128]{3,2,1,0:T(8,128)S(1)} %bitcast.72, f32[128]{0:T(128)S(1)} %copy-done.9, f32[128,4,8]{0,2,1:T(8,128)S(1)} %rsqrt_bitcast_fusion, bf16[512,4,128,1]{2,1,0,3:T(4,128)(2,1)S(1)} %bitcast.76), kind=kOutput, calls=%fused_computation.1 | convolution fusion | flops 544731136 | bytes 11108864 | tf_op jit(solution)/shard_map/tgrd,pgd->grtp/dot_general | solution.py:74
  180.6 1.8 fusion.12
  182.3 1.3 copy.85
  (47 shorter events, 3.2 us)
Async XLA Ops:
  6.5 28.6 %copy-start = (bf16[512,1024]{1,0:T(8,128)(2,1)S(1)}, bf16[512,1024]{1,0:T(8,128)(2,1)}, u32[]{:S(2)}) copy-start(bf16[512,1024]{1,0:T(8,128)(2,1)} %param.9) | copy-start | bytes 3145732
  6.5 97.0 %reduce-scatter.2.cloned.1.call-start = ((), (), s32[]{:S(2)}) async-start(), calls=%async_computation.2 | async-start | bytes 3342336 | tf_op jit(solution)/shard_map/reduce_scatter | solution.py:25
  37.8 0.7 copy-start.6
  106.6 1.6 collective-permute-start
  108.2 9.3 %copy-start.7 = (s32[3]{0:T(128)S(1)}, s32[3]{0:T(128)}, u32[]{:S(2)}) copy-start(s32[3]{0:T(128)} %param.12) | copy-start | bytes 40
  108.2 10.0 %copy-start.8 = (s32[3]{0:T(128)S(1)}, s32[3]{0:T(128)}, u32[]{:S(2)}) copy-start(s32[3]{0:T(128)} %param.13) | copy-start | bytes 40
  108.2 7.4 %collective-permute-start.1 = (bf16[96,1024]{1,0:T(8,128)(2,1)S(1)}, bf16[96,1024]{1,0:T(8,128)(2,1)S(1)}, u32[]{:S(2)}, u32[]{:S(2)}) collective-permute-start(bf16[96,1024]{1,0:T(8,128)(2,1)S(1)} %maximum_select_fusion.3), channel_id=1, source_target_pairs={{0,2},{1,3},{2,0},{3,1},{4,6},{5,7},{6,4},{7,5},{8,10},{9,11},{10,... | collective-permute-start | bytes 589832 | tf_op jit(solution)/shard_map/ppermute | solution.py:54
  115.7 10.8 %collective-permute-start.2 = (bf16[192,1024]{1,0:T(8,128)(2,1)S(1)}, bf16[192,1024]{1,0:T(8,128)(2,1)}, u32[]{:S(2)}, u32[]{:S(2)}) collective-permute-start(bf16[192,1024]{1,0:T(8,128)(2,1)S(1)} %maximum_select_fusion.2), channel_id=1, source_target_pairs={{0,4},{1,5},{2,6},{3,7},{4,0},{5,1},{6,2},{7,3},{8,12},{9,13},{10,... | collective-permute-start | bytes 1179656 | tf_op jit(solution)/shard_map/ppermute | solution.py:54
  120.6 3.9 %copy-start.1 = (f32[16,8,32,128]{3,1,2,0:T(8,128)S(1)}, f32[16,8,32,128]{3,1,2,0:T(8,128)}, u32[]{:S(2)}) copy-start(f32[16,8,32,128]{3,1,2,0:T(8,128)} %convert_bitcast_fusion) | copy-start | bytes 6291460
  124.4 1.8 copy-start.10
  124.5 1.7 copy-start.11
  124.5 1.8 copy-start.5
  128.0 36.5 %collective-permute-start.3 = (bf16[384,1024]{1,0:T(8,128)(2,1)S(1)}, bf16[384,1024]{1,0:T(8,128)(2,1)S(1)}, u32[]{:S(2)}, u32[]{:S(2)}) collective-permute-start(bf16[384,1024]{1,0:T(8,128)(2,1)S(1)} %maximum_select_fusion.1), channel_id=1, source_target_pairs={{0,8},{1,9},{2,10},{3,11},{4,12},{5,13},{6,14},{7,15},{8,0},{9,1},... | collective-permute-start | bytes 2359304 | tf_op jit(solution)/shard_map/ppermute | solution.py:54
  167.0 6.0 %copy-start.2 = (f32[16,8,32,128]{3,2,1,0:T(8,128)S(1)}, f32[16,8,32,128]{3,2,1,0:T(8,128)}, u32[]{:S(2)}) copy-start(f32[16,8,32,128]{3,2,1,0:T(8,128)} %copy.100) | copy-start | bytes 6291460
  167.0 6.0 %copy-start.9 = (f32[128]{0:T(128)S(1)}, f32[128]{0:T(128)}, u32[]{:S(2)}) copy-start(f32[128]{0:T(128)} %param.10) | copy-start | bytes 1540
  176.2 1.0 copy-start.3
  177.3 3.3 %copy-start.4 = (bf16[512,512]{0,1:T(8,128)(2,1)S(1)}, bf16[512,512]{0,1:T(8,128)(2,1)}, u32[]{:S(2)}) copy-start(bf16[512,512]{0,1:T(8,128)(2,1)} %copy.94) | copy-start | bytes 1572868
Sparse Core Ops, SparseCore 0:
  38.0 65.5 reduce-scatter.1
